TPU v7x, 32 devices: a whole 2x2x4 slice. The times are simulated.
32 devices in a mesh: seq: 8 (over z, x), chan: 4 (over y, core).
Axes of the slice: x: 2, y: 2, z: 4, core: 2. Of those that a mesh axis runs over, the one named last changes fastest.
Arguments:
- query: bfloat16 [2048, 4096], P('seq', 'chan'), may hold values from -6 to 6
- key_gate: bfloat16 [2048, 4096], P('seq', 'chan'), may hold values from -6 to 6
- value: bfloat16 [2048, 4096], P('seq', 'chan'), may hold values from -6 to 6
- group_order: int32 [16], replicated, may hold values from 0 to 15, each once
- emb_weight: float32 [33, 64], replicated, may hold values from -32 to 32
- emb_bias: float32 [64], replicated, may hold values from -1 to 1
- mid_weight: float32 [64, 64], replicated, may hold values from -0.75 to 0.75
- mid_bias: float32 [64], replicated, may hold values from -1 to 1
- out_filter: float32 [64, 4096], P(None, 'chan'), may hold values from -0.75 to 0.75
- decay_rate: float32 [4096], P('chan'), may hold values from 0.00014648438 to 0.0014648438
- skip_gain: float32 [4096], P('chan'), may hold values from 0.5 to 1.5
- out_weight: bfloat16 [4096, 4096], P('chan'), may hold values from -0.125 to 0.125
Outputs:
- projected: float32 [4096, 2048], P('chan', 'seq')
Inputs may be any that keep to these rules, and one draw needn't show every extreme that they name: `group_order`: a permutation of the group numbers.
All inputs are finite; a program needn't handle non-finite values.
Results may differ from a plain program's by a relative error of at most 0.011.
Values may be sent and summed in bfloat16 or wider, within the bound.
No kernel may reach another device: no remote copies, remote signals or barrier semaphores. Data moves between devices by JAX's collectives and lax.ppermute only.
A program may use at most 128 MiB of HBM per device.

v0:
```python
import math
import jax
import jax.numpy as jnp
from jax import lax
from jax.sharding import PartitionSpec as P

BLOCK = 128
sine_freq = 2.0


def transform_tables(block):
    period = 2 * block
    row_index = jnp.arange(block, dtype=jnp.int32)
    freq_index = jnp.arange(block + 1, dtype=jnp.int32)
    scale = math.pi / block
    angle_head = (freq_index[:, None] * row_index[None, :] % period).astype(jnp.float32) * scale
    fwd_head = jnp.concatenate([jnp.cos(angle_head), -jnp.sin(angle_head)], 0).astype(jnp.bfloat16)
    angle_tail = (freq_index[:, None] * (row_index[None, :] + block) % period).astype(
        jnp.float32
    ) * scale
    keep_cols = (row_index > 0).astype(jnp.float32)[None, :]
    fwd_tail = (jnp.concatenate([jnp.cos(angle_tail), -jnp.sin(angle_tail)], 0) * keep_cols).astype(
        jnp.bfloat16
    )
    weights = (
        jnp.where((freq_index == 0) | (freq_index == block), 1.0, 2.0).astype(jnp.float32) / period
    )
    angle_back = (row_index[:, None] * freq_index[None, :] % period).astype(jnp.float32) * scale
    inverse = jnp.concatenate(
        [jnp.cos(angle_back) * weights[None, :], -jnp.sin(angle_back) * weights[None, :]], 1
    ).astype(jnp.bfloat16)
    return (fwd_head, fwd_tail, inverse)


def filter_rows(
    positions, length, emb_weight, emb_bias, mid_weight, mid_bias, out_filter, decay_rate
):
    high = lax.Precision.HIGHEST
    time_float = positions.astype(jnp.float32)
    band_count = (emb_weight.shape[0] - 1) // 2
    band_index = jnp.arange(1, band_count + 1, dtype=jnp.int32)
    angles = (positions[:, None] * band_index[None, :] % length).astype(jnp.float32) * (
        2.0 * math.pi / length
    )
    embedded = jnp.concatenate([time_float[:, None] / length, jnp.cos(angles), jnp.sin(angles)], 1)
    hidden = jnp.sin(
        sine_freq * (jnp.dot(embedded, emb_weight, precision=high) + emb_bias[None, :])
    )
    hidden = jnp.sin(sine_freq * (jnp.dot(hidden, mid_weight, precision=high) + mid_bias[None, :]))
    filter_raw = jnp.dot(hidden, out_filter, precision=high)
    norm_scale = jnp.sqrt(-jnp.expm1(-2.0 * decay_rate))
    decayed = jnp.exp(-decay_rate[None, :] * time_float[:, None])
    return (filter_raw * decayed * norm_scale[None, :]).astype(jnp.bfloat16)


def local(
    query,
    key_gate,
    value,
    group_order,
    emb_weight,
    emb_bias,
    mid_weight,
    mid_bias,
    out_filter,
    decay_rate,
    skip_gain,
    out_weight,
):
    tok_rows, chan_width = query.shape
    my_groups = tok_rows // BLOCK
    seq_count = lax.axis_size("seq")
    length = tok_rows * seq_count
    total_groups = length // BLOCK
    half_rows = BLOCK + 1
    fwd_head, fwd_tail, inverse = transform_tables(BLOCK)
    seq_index = lax.axis_index("seq")
    mine = lax.dynamic_slice_in_dim(group_order, seq_index * my_groups, my_groups)
    signal = (key_gate.astype(jnp.float32) * value.astype(jnp.float32)).astype(jnp.bfloat16)
    positions = seq_index * tok_rows + jnp.arange(tok_rows, dtype=jnp.int32)
    own_rows = filter_rows(
        positions, length, emb_weight, emb_bias, mid_weight, mid_bias, out_filter, decay_rate
    )
    whole_filter = lax.all_gather(own_rows, "seq", axis=0, tiled=True)
    blocks = whole_filter.reshape(total_groups, BLOCK, chan_width)
    previous = jnp.concatenate([jnp.zeros((1, BLOCK, chan_width), jnp.bfloat16), blocks[:-1]], 0)

    def block_spectrum(blocks_pair):
        head_part = jnp.dot(fwd_head, blocks_pair[0], preferred_element_type=jnp.float32)
        tail_part = jnp.dot(fwd_tail, blocks_pair[1], preferred_element_type=jnp.float32)
        return (head_part + tail_part).astype(jnp.bfloat16)

    filter_spectrum = lax.map(block_spectrum, (blocks, previous))

    def accumulate(spectra_sum, spectrum, global_id):
        lag_index = mine - global_id
        causal = (lag_index >= 0).astype(jnp.float32)[:, None, None]
        picked = filter_spectrum[jnp.maximum(lag_index, 0)]
        filt_real = picked[:, :half_rows].astype(jnp.float32)
        filt_imag = picked[:, half_rows:].astype(jnp.float32)
        sig_real = spectrum[None, :half_rows].astype(jnp.float32)
        sig_imag = spectrum[None, half_rows:].astype(jnp.float32)
        real_part = filt_real * sig_real - filt_imag * sig_imag
        imag_part = filt_real * sig_imag + filt_imag * sig_real
        return spectra_sum + causal * jnp.concatenate([real_part, imag_part], 1)

    empty = jnp.zeros((my_groups, 2 * half_rows, chan_width), jnp.float32)

    def advance(running, element):
        spectrum = jnp.dot(fwd_head, element[0], preferred_element_type=jnp.float32).astype(
            jnp.bfloat16
        )
        return (accumulate(running, spectrum, element[1]), None)

    running, _ = lax.scan(
        advance,
        empty,
        (
            lax.all_gather(signal.reshape(my_groups, BLOCK, chan_width), "seq", axis=0, tiled=True),
            group_order,
        ),
    )
    out_spectrum = running.astype(jnp.bfloat16)
    convolved = jnp.einsum(
        "rk,nkc->nrc", inverse, out_spectrum, preferred_element_type=jnp.float32
    ).reshape(tok_rows, chan_width)
    mixed = (
        query.astype(jnp.float32) * (convolved + skip_gain[None, :] * signal.astype(jnp.float32))
    ).astype(jnp.bfloat16)
    return lax.psum_scatter(
        lax.dot_general(
            out_weight, mixed, (((0,), (1,)), ((), ())), preferred_element_type=jnp.float32
        ).astype(jnp.bfloat16),
        "chan",
        scatter_dimension=0,
        tiled=True,
    ).astype(jnp.float32)


def solution(mesh):
    return jax.shard_map(
        local,
        mesh=mesh,
        in_specs=(
            P("seq", "chan"),
            P("seq", "chan"),
            P("seq", "chan"),
            P(),
            P(),
            P(),
            P(),
            P(),
            P(None, "chan"),
            P("chan"),
            P("chan"),
            P("chan", None),
        ),
        out_specs=P("chan", "seq"),
        check_vma=False,
    )
```

profile of v0, /device:TPU:0, one launch (start us, length us, event | category | flops | bytes accessed | tf_op | source)
XLA Modules:
  0.0 414.4 jit_solution(10690862169828464235)
XLA Ops:
  7.5 1.5 fusion.23
  9.1 1.4 fusion.21
  10.5 1.9 fusion.19
  14.6 74.0 %all-gather.3.cloned.1.call-done = bf16[2048,1024]{1,0:T(8,128)(2,1)} async-done(((bf16[256,1024]{1,0:T(8,128)(2,1)}), bf16[2048,1024]{1,0:T(8,128)(2,1)}) %all-gather.3.cloned.1.call-update) | async-done | bytes 4194320 | tf_op jit(solution)/shard_map/all_gather | solution.py:84
  88.7 2.1 slice-done
  90.8 2.4 concatenate.22
  93.2 53.1 %while.21 = (s32[]{:T(128)}, bf16[16,258,1024]{2,1,0:T(8,128)(2,1)}, bf16[16,128,1024]{2,1,0:T(8,128)(2,1)}, bf16[258,128]{1,0:T(8,128)(2,1)S(1)}, bf16[16,128,1...) while((s32[]{:T(128)}, bf16[16,258,1024]{2,1,0:T(8,128)(2,1)}, ...), condition=%wide.region_1.2_spmd, body=%wide.region_0.1_spmd.sunk | while | flops 135794688 | bytes 3312205 | solution.py:93
  94.4 2.1 fusion.91
  97.8 2.1 fusion.91
  101.1 2.1 fusion.91
  104.4 2.1 fusion.91
  107.7 2.1 fusion.91
  111.0 2.0 fusion.91
  114.3 2.1 fusion.91
  117.6 2.1 fusion.91
  120.9 2.1 fusion.91
  124.3 2.1 fusion.91
  127.6 2.1 fusion.91
  130.9 2.1 fusion.91
  134.2 2.1 fusion.91
  137.6 2.0 fusion.91
  140.8 2.1 fusion.91
  144.2 2.1 fusion.91
  146.3 16.2 %all-gather.5.cloned.1.call-done = bf16[16,128,1024]{2,1,0:T(8,128)(2,1)} async-done(((bf16[2,128,1024]{2,1,0:T(8,128)(2,1)}), bf16[16,128,1024]{2,1,0:T(8,128)(2,1)}) %all-gather.5.cloned.1.call-update) | async-done | bytes 4194320 | tf_op jit(solution)/shard_map/all_gather | solution.py:119
  162.5 203.8 %while.22 = (s32[]{:T(128)}, f32[2,258,1024]{2,1,0:T(8,128)}, s32[16]{0:T(128)S(1)}, s32[2]{0:T(128)S(1)}, bf16[16,258,1024]{2,1,0:T(8,128)(2,1)}, /*index=5*/bf...) while((s32[]{:T(128)}, f32[2,258,1024]{2,1,0:T(8,128)}, ...), condition=%wide.region_3.4_spmd.clone, body=%wide.region_2.3_spmd.clone.sunk | while | flops 72389640 | bytes 15127731 | solution.py:115
  163.7 4.1 gather_fusion
  171.2 3.3 fusion.96
  175.8 4.1 gather_fusion
  183.3 4.0 fusion.96
  188.6 4.1 gather_fusion
  196.1 4.0 fusion.96
  201.4 4.1 gather_fusion
  208.9 4.0 fusion.96
  214.1 4.1 gather_fusion
  221.7 4.0 fusion.96
  226.9 4.1 gather_fusion
  234.4 4.0 fusion.96
  239.7 4.1 gather_fusion
  245.2 1.4 fusion.95
  247.2 4.0 fusion.96
  252.5 4.1 gather_fusion
  260.0 4.0 fusion.96
  265.3 4.1 gather_fusion
  272.8 4.0 fusion.96
  278.0 4.1 gather_fusion
  285.6 4.0 fusion.96
  290.8 4.1 gather_fusion
  298.3 4.0 fusion.96
  303.6 4.1 gather_fusion
  311.1 4.0 fusion.96
  316.4 4.1 gather_fusion
  321.8 1.4 fusion.95
  323.9 4.0 fusion.96
  329.2 4.1 gather_fusion
  334.6 1.4 fusion.95
  336.7 4.0 fusion.96
  341.9 4.1 gather_fusion
  349.5 4.0 fusion.96
  354.7 4.1 gather_fusion
  362.2 4.0 fusion.96
  366.3 2.2 fusion.24
  368.7 7.1 %fusion.17 = bf16[4096,256]{0,1:T(8,128)(2,1)} fusion(bf16[256,1024]{1,0:T(8,128)(2,1)S(1)} %fusion.27, bf16[1024,4096]{1,0:T(8,128)(2,1)} %param.27), kind=kOutput, calls=%fused_computation.31 | convolution fusion | flops 2148532224 | bytes 11010048 | tf_op jit(solution)/shard_map/dot_general | solution.py:131
  375.8 29.8 %reduce-scatter.2.cloned.1.call-done = bf16[1024,256]{0,1:T(8,128)(2,1)} async-done(((bf16[4096,256]{0,1:T(8,128)(2,1)}), bf16[1024,256]{0,1:T(8,128)(2,1)}) %reduce-scatter.2.cloned.1.call-update) | async-done | bytes 524304 | tf_op jit(solution)/shard_map/reduce_scatter | solution.py:130
  405.7 2.2 copy.14
  (164 shorter events, 93.3 us)
Async XLA Ops:
  6.5 4.0 copy-start
  6.5 5.9 %copy-start.3 = (bf16[256,1024]{1,0:T(8,128)(2,1)S(1)}, bf16[256,1024]{1,0:T(8,128)(2,1)}, u32[]{:S(2)}) copy-start(bf16[256,1024]{1,0:T(8,128)(2,1)} %param.17) | copy-start | bytes 1572868
  6.5 5.9 %copy-start.2 = (bf16[256,1024]{1,0:T(8,128)(2,1)S(1)}, bf16[256,1024]{1,0:T(8,128)(2,1)}, u32[]{:S(2)}) copy-start(bf16[256,1024]{1,0:T(8,128)(2,1)} %param.18) | copy-start | bytes 1572868
  6.5 82.1 %all-gather.3.cloned.1.call-start = ((), (), s32[]{:S(2)}) async-start(), calls=%async_computation.1 | async-start | bytes 4718592 | tf_op jit(solution)/shard_map/all_gather | solution.py:84
  10.5 4.0 copy-start.6
  12.4 150.1 %all-gather.5.cloned.1.call-start = ((), (), s32[]{:S(2)}) async-start(), calls=%async_computation.2 | async-start | bytes 4718592 | tf_op jit(solution)/shard_map/all_gather | solution.py:119
  13.5 392.2 %reduce-scatter.2.cloned.1.call-start = ((), (), s32[]{:S(2)}) async-start(), calls=%async_computation.3 | async-start | bytes 2621440 | tf_op jit(solution)/shard_map/reduce_scatter | solution.py:130
  88.7 2.1 slice-start
  366.3 2.2 copy-start.1
  366.3 2.2 copy-start.4
  366.3 2.2 copy-start.5
Sparse Core Ops, SparseCore 0:
  12.5 76.0 all-gather.2
  90.8 71.6 all-gather.4
  375.9 29.6 reduce-scatter.1
where the time goes:
time: 417 us; the launch traced here: 414 us
  waiting for transfers between devices  120 us (29%)
  other arithmetic  112 us (27%)
  matrix products  87 us (21%)
  local copies, waits for them, and re-layouts  81.3 us (19%)
  between operations  13.3 us (3%)
    all_gather x1, waiting for transfers between devices, local(): whole_filter = lax.all_gather(own_rows, 'seq', axis=0, tiled=True)  74 us
    gather x16, local copies, waits for them, and re-layouts, accumulate(): picked = filter_spectrum[jnp.maximum(lag_index, 0)]  65.2 us
    add x16, other arithmetic, accumulate(): return spectra_sum + causal * jnp.concatenate([real_part, imag_part], 1)  63.5 us
    dot_general x16, matrix products, block_spectrum(): jnp.dot(fwd_tail, blocks_pair[1], preferred_element_type=jnp.float32)  33.1 us
    reduce_scatter x1, waiting for transfers between devices, local(): lax.psum_scatter(lax.dot_general(out_weight, mixed, (((0,), (1,)), ((), (...  29.8 us
    sub x16, other arithmetic, accumulate(): real_part = filt_real * sig_real - filt_imag * sig_imag  22.4 us
    dot_general x16, matrix products, advance(): jnp.dot(fwd_head, element[0], preferred_element_type=jnp.float32)  19.9 us
    dot_general x16, matrix products, block_spectrum(): jnp.dot(fwd_head, blocks_pair[0], preferred_element_type=jnp.float32)  19.9 us
  transfers between devices with their start and end apart: 3, of which 3 were waited for; matrix products, arithmetic and copies ran while one was open for 14% of the time, Pallas kernels for 0%

commit v1 on v0

--- a/solution.py
+++ b/solution.py
@@ -81,7 +81,12 @@
     own_rows = filter_rows(
         positions, length, emb_weight, emb_bias, mid_weight, mid_bias, out_filter, decay_rate
     )
-    whole_filter = lax.all_gather(own_rows, "seq", axis=0, tiled=True)
+    ring = [own_rows]
+    for hop in range(7):
+        ring.append(lax.ppermute(ring[-1], "seq", [(dev, (dev + 1) % 8) for dev in range(8)]))
+    whole_filter = jnp.roll(
+        jnp.concatenate(ring[::-1], axis=0), (lax.axis_index("seq") + 1) * ring[0].shape[0], axis=0
+    )
     blocks = whole_filter.reshape(total_groups, BLOCK, chan_width)
     previous = jnp.concatenate([jnp.zeros((1, BLOCK, chan_width), jnp.bfloat16), blocks[:-1]], 0)
 

time: 417 us -> 440 us (1.055)
  waiting for transfers between devices: 120 us -> 136 us
    ppermute x0 -> x7, waiting for transfers between devices: none -> 108 us  [local(): lax.ppermute(ring[-1], 'seq', [(dev, (dev + 1) % 8) for dev in range(8)])]
    all_gather x1 -> x0, waiting for transfers between devices: 74 us -> none  [local(): whole_filter = lax.all_gather(own_rows, 'seq', axis=0, tiled=True)]
    all_gather x1, waiting for transfers between devices: 16.2 us -> 0.01 us  [local(): lax.all_gather(signal.reshape(my_groups, BLOCK, chan_width), 'seq', axis=...]
  transfers between devices with their start and end apart: 3 -> 9, of which waited for: 3 -> 8; matrix products, arithmetic and copies ran while one was open for 14% -> 14% of each run, Pallas kernels for 0% -> 0%
where the time goes in v1:
time: 440 us; the launch traced here: 436 us
  waiting for transfers between devices  136 us (31%)
  other arithmetic  113 us (26%)
  matrix products  85.9 us (20%)
  local copies, waits for them, and re-layouts  83.3 us (19%)
  between operations  13.7 us (3%)
    ppermute x7, waiting for transfers between devices, local(): lax.ppermute(ring[-1], 'seq', [(dev, (dev + 1) % 8) for dev in range(8)])  108 us
    gather x16, local copies, waits for them, and re-layouts, accumulate(): picked = filter_spectrum[jnp.maximum(lag_index, 0)]  65.2 us
    add x16, other arithmetic, accumulate(): return spectra_sum + causal * jnp.concatenate([real_part, imag_part], 1)  63.6 us
    dot_general x16, matrix products, block_spectrum(): jnp.dot(fwd_tail, blocks_pair[1], preferred_element_type=jnp.float32)  33 us
    reduce_scatter x1, waiting for transfers between devices, local(): lax.psum_scatter(lax.dot_general(out_weight, mixed, (((0,), (1,)), ((), (...  27.7 us
    sub x16, other arithmetic, accumulate(): real_part = filt_real * sig_real - filt_imag * sig_imag  22 us
    dot_general x16, matrix products, advance(): jnp.dot(fwd_head, element[0], preferred_element_type=jnp.float32)  19.9 us
    dot_general x16, matrix products, block_spectrum(): jnp.dot(fwd_head, blocks_pair[0], preferred_element_type=jnp.float32)  19.8 us
  transfers between devices with their start and end apart: 9, of which 8 were waited for; matrix products, arithmetic and copies ran while one was open for 14% of the time, Pallas kernels for 0%

profile of v1, /device:TPU:0, one launch (start us, length us, event | category | flops | bytes accessed | tf_op | source)
XLA Modules:
  0.0 436.5 jit_solution(3652854996209632523)
XLA Ops:
  11.5 3.0 collective-permute-start
  14.5 15.0 %collective-permute-done = bf16[256,1024]{1,0:T(8,128)(2,1)S(1)} collective-permute-done((bf16[256,1024]{1,0:T(8,128)(2,1)S(1)}, bf16[256,1024]{1,0:T(8,128)(2,1)S(1)}, u32[]{:S(2)}, u32[]{:S(2)}) %collective-permute-start) | collective-permute-done | bytes 524320 | tf_op jit(solution)/shard_map/ppermute | solution.py:86
  29.5 15.8 %collective-permute-done.1 = bf16[256,1024]{1,0:T(8,128)(2,1)S(1)} collective-permute-done((bf16[256,1024]{1,0:T(8,128)(2,1)S(1)}, bf16[256,1024]{1,0:T(8,128)(2,1)S(1)}, u32[]{:S(2)}, u32[]{:S(2)}) %collective-permute-start.1) | collective-permute-done | bytes 524320 | tf_op jit(solution)/shard_map/ppermute | solution.py:86
  45.3 14.9 %collective-permute-done.2 = bf16[256,1024]{1,0:T(8,128)(2,1)S(1)} collective-permute-done((bf16[256,1024]{1,0:T(8,128)(2,1)S(1)}, bf16[256,1024]{1,0:T(8,128)(2,1)S(1)}, u32[]{:S(2)}, u32[]{:S(2)}) %collective-permute-start.2) | collective-permute-done | bytes 524320 | tf_op jit(solution)/shard_map/ppermute | solution.py:86
  60.2 14.0 %collective-permute-done.3 = bf16[256,1024]{1,0:T(8,128)(2,1)S(1)} collective-permute-done((bf16[256,1024]{1,0:T(8,128)(2,1)S(1)}, bf16[256,1024]{1,0:T(8,128)(2,1)S(1)}, u32[]{:S(2)}, u32[]{:S(2)}) %collective-permute-start.3) | collective-permute-done | bytes 524320 | tf_op jit(solution)/shard_map/ppermute | solution.py:86
  74.1 2.2 multiply_convert_fusion
  77.2 10.0 %collective-permute-done.4 = bf16[256,1024]{1,0:T(8,128)(2,1)S(1)} collective-permute-done((bf16[256,1024]{1,0:T(8,128)(2,1)S(1)}, bf16[256,1024]{1,0:T(8,128)(2,1)S(1)}, u32[]{:S(2)}, u32[]{:S(2)}) %collective-permute-start.4) | collective-permute-done | bytes 524320 | tf_op jit(solution)/shard_map/ppermute | solution.py:86
  87.8 26.3 %collective-permute-done.5 = bf16[256,1024]{1,0:T(8,128)(2,1)S(1)} collective-permute-done((bf16[256,1024]{1,0:T(8,128)(2,1)S(1)}, bf16[256,1024]{1,0:T(8,128)(2,1)S(1)}, u32[]{:S(2)}, u32[]{:S(2)}) %collective-permute-start.5) | collective-permute-done | bytes 524320 | tf_op jit(solution)/shard_map/ppermute | solution.py:86
  115.1 12.5 %collective-permute-done.6 = bf16[256,1024]{1,0:T(8,128)(2,1)S(1)} collective-permute-done((bf16[256,1024]{1,0:T(8,128)(2,1)S(1)}, bf16[256,1024]{1,0:T(8,128)(2,1)S(1)}, u32[]{:S(2)}, u32[]{:S(2)}) %collective-permute-start.6) | collective-permute-done | bytes 524320 | tf_op jit(solution)/shard_map/ppermute | solution.py:86
  128.7 2.4 constant_dynamic-slice_fusion.1
  131.1 2.4 concatenate.29
  133.5 53.0 %while.21 = (s32[]{:T(128)}, bf16[16,258,1024]{2,1,0:T(8,128)(2,1)}, bf16[16,128,1024]{2,1,0:T(8,128)(2,1)}, bf16[258,128]{1,0:T(8,128)(2,1)S(1)}, bf16[16,128,1...) while((s32[]{:T(128)}, bf16[16,258,1024]{2,1,0:T(8,128)(2,1)}, ...), condition=%wide.region_1.2_spmd, body=%wide.region_0.1_spmd.sunk | while | flops 135794688 | bytes 3312205 | solution.py:98
  134.8 2.1 fusion.91
  138.1 2.1 fusion.91
  141.4 2.1 fusion.91
  144.7 2.0 fusion.91
  148.0 2.1 fusion.91
  151.3 2.0 fusion.91
  154.6 2.1 fusion.91
  157.9 2.0 fusion.91
  161.2 2.1 fusion.91
  164.5 2.1 fusion.91
  167.8 2.0 fusion.91
  171.1 2.1 fusion.91
  174.4 2.1 fusion.91
  181.0 2.1 fusion.91
  184.4 2.1 fusion.91
  186.5 202.6 %while.22 = (s32[]{:T(128)}, f32[2,258,1024]{2,1,0:T(8,128)}, s32[16]{0:T(128)S(1)}, s32[2]{0:T(128)S(1)}, bf16[16,258,1024]{2,1,0:T(8,128)(2,1)}, /*index=5*/bf...) while((s32[]{:T(128)}, f32[2,258,1024]{2,1,0:T(8,128)}, ...), condition=%wide.region_3.4_spmd.clone, body=%wide.region_2.3_spmd.clone.sunk | while | flops 72389640 | bytes 15127731 | solution.py:120
  187.8 4.1 gather_fusion
  195.2 3.3 fusion.96
  199.8 4.1 gather_fusion
  207.2 4.0 fusion.96
  212.5 4.1 gather_fusion
  219.9 4.0 fusion.96
  225.2 4.1 gather_fusion
  232.6 4.0 fusion.96
  237.9 4.1 gather_fusion
  245.3 4.0 fusion.96
  250.6 4.1 gather_fusion
  258.0 4.0 fusion.96
  263.3 4.1 gather_fusion
  270.8 4.0 fusion.96
  276.0 4.1 gather_fusion
  283.5 4.0 fusion.96
  288.7 4.1 gather_fusion
  296.2 4.0 fusion.96
  301.4 4.1 gather_fusion
  308.9 4.0 fusion.96
  314.1 4.1 gather_fusion
  321.6 4.0 fusion.96
  326.8 4.1 gather_fusion
  334.3 4.0 fusion.96
  339.5 4.1 gather_fusion
  347.0 4.0 fusion.96
  352.2 4.1 gather_fusion
  359.7 4.0 fusion.96
  365.0 4.1 gather_fusion
  372.4 4.0 fusion.96
  377.7 4.1 gather_fusion
  385.1 4.0 fusion.96
  389.1 2.1 fusion.24
  392.6 7.0 %fusion.17 = bf16[4096,256]{0,1:T(8,128)(2,1)} fusion(bf16[256,1024]{1,0:T(8,128)(2,1)S(1)} %fusion.27, bf16[1024,4096]{1,0:T(8,128)(2,1)} %param.27), kind=kOutput, calls=%fused_computation.31 | convolution fusion | flops 2148532224 | bytes 11010048 | tf_op jit(solution)/shard_map/dot_general | solution.py:136
  399.7 27.7 %reduce-scatter.2.cloned.1.call-done = bf16[1024,256]{0,1:T(8,128)(2,1)} async-done(((bf16[4096,256]{0,1:T(8,128)(2,1)}), bf16[1024,256]{0,1:T(8,128)(2,1)}) %reduce-scatter.2.cloned.1.call-update) | async-done | bytes 524304 | tf_op jit(solution)/shard_map/reduce_scatter | solution.py:135
  427.4 2.2 copy.14
  (189 shorter events, 104.6 us)
Async XLA Ops:
  6.5 3.9 copy-start
  6.5 179.9 %all-gather.2.cloned.1.call-start = ((), (), s32[]{:S(2)}) async-start(), calls=%async_computation.1 | async-start | bytes 4718592 | tf_op jit(solution)/shard_map/all_gather | solution.py:124
  11.5 18.0 %collective-permute-start = (bf16[256,1024]{1,0:T(8,128)(2,1)S(1)}, bf16[256,1024]{1,0:T(8,128)(2,1)S(1)}, u32[]{:S(2)}, u32[]{:S(2)}) collective-permute-start(bf16[256,1024]{1,0:T(8,128)(2,1)S(1)} %fusion.19), channel_id=1, source_target_pairs={{0,4},{4,8},{8,12},{12,16},{16,20},{20,24},{24,28},{28,0},{1,5},{5... | collective-permute-start | bytes 1572872 | tf_op jit(solution)/shard_map/ppermute | solution.py:86
  29.5 15.8 %collective-permute-start.1 = (bf16[256,1024]{1,0:T(8,128)(2,1)S(1)}, bf16[256,1024]{1,0:T(8,128)(2,1)S(1)}, u32[]{:S(2)}, u32[]{:S(2)}) collective-permute-start(bf16[256,1024]{1,0:T(8,128)(2,1)S(1)} %collective-permute-done), channel_id=1, source_target_pairs={{0,4},{4,8},{8,12},{12,16},{16,20},{20,24},{24,28},{28,0},{1,5},{5... | collective-permute-start | bytes 1572872 | tf_op jit(solution)/shard_map/ppermute | solution.py:86
  45.3 14.9 %collective-permute-start.2 = (bf16[256,1024]{1,0:T(8,128)(2,1)S(1)}, bf16[256,1024]{1,0:T(8,128)(2,1)S(1)}, u32[]{:S(2)}, u32[]{:S(2)}) collective-permute-start(bf16[256,1024]{1,0:T(8,128)(2,1)S(1)} %collective-permute-done.1), channel_id=1, source_target_pairs={{0,4},{4,8},{8,12},{12,16},{16,20},{20,24},{24,28},{28,0},{1,5},{5... | collective-permute-start | bytes 1572872 | tf_op jit(solution)/shard_map/ppermute | solution.py:86
  60.2 14.0 %collective-permute-start.3 = (bf16[256,1024]{1,0:T(8,128)(2,1)S(1)}, bf16[256,1024]{1,0:T(8,128)(2,1)S(1)}, u32[]{:S(2)}, u32[]{:S(2)}) collective-permute-start(bf16[256,1024]{1,0:T(8,128)(2,1)S(1)} %collective-permute-done.2), channel_id=1, source_target_pairs={{0,4},{4,8},{8,12},{12,16},{16,20},{20,24},{24,28},{28,0},{1,5},{5... | collective-permute-start | bytes 1572872 | tf_op jit(solution)/shard_map/ppermute | solution.py:86
  74.1 13.0 %collective-permute-start.4 = (bf16[256,1024]{1,0:T(8,128)(2,1)S(1)}, bf16[256,1024]{1,0:T(8,128)(2,1)S(1)}, u32[]{:S(2)}, u32[]{:S(2)}) collective-permute-start(bf16[256,1024]{1,0:T(8,128)(2,1)S(1)} %collective-permute-done.3), channel_id=1, source_target_pairs={{0,4},{4,8},{8,12},{12,16},{16,20},{20,24},{24,28},{28,0},{1,5},{5... | collective-permute-start | bytes 1572872 | tf_op jit(solution)/shard_map/ppermute | solution.py:86
  76.3 351.1 %reduce-scatter.2.cloned.1.call-start = ((), (), s32[]{:S(2)}) async-start(), calls=%async_computation.2 | async-start | bytes 2621440 | tf_op jit(solution)/shard_map/reduce_scatter | solution.py:135
  87.2 26.9 %collective-permute-start.5 = (bf16[256,1024]{1,0:T(8,128)(2,1)S(1)}, bf16[256,1024]{1,0:T(8,128)(2,1)S(1)}, u32[]{:S(2)}, u32[]{:S(2)}) collective-permute-start(bf16[256,1024]{1,0:T(8,128)(2,1)S(1)} %collective-permute-done.4), channel_id=1, source_target_pairs={{0,4},{4,8},{8,12},{12,16},{16,20},{20,24},{24,28},{28,0},{1,5},{5... | collective-permute-start | bytes 1572872 | tf_op jit(solution)/shard_map/ppermute | solution.py:86
  114.1 13.5 %collective-permute-start.6 = (bf16[256,1024]{1,0:T(8,128)(2,1)S(1)}, bf16[256,1024]{1,0:T(8,128)(2,1)S(1)}, u32[]{:S(2)}, u32[]{:S(2)}) collective-permute-start(bf16[256,1024]{1,0:T(8,128)(2,1)S(1)} %collective-permute-done.5), channel_id=1, source_target_pairs={{0,4},{4,8},{8,12},{12,16},{16,20},{20,24},{24,28},{28,0},{1,5},{5... | collective-permute-start | bytes 1572872 | tf_op jit(solution)/shard_map/ppermute | solution.py:86
  133.5 53.0 %copy-start.5 = (s32[16]{0:T(128)S(1)}, s32[16]{0:T(128)}, u32[]{:S(2)}) copy-start(s32[16]{0:T(128)} %param.19) | copy-start | bytes 196
  186.5 202.7 %copy-start.2 = (bf16[128,129]{0,1:T(8,128)(2,1)S(1)}, bf16[128,129]{0,1:T(8,128)(2,1)}, u32[]{:S(2)}) copy-start(bf16[128,129]{0,1:T(8,128)(2,1)} %get-tuple-element.134) | copy-start | bytes 99076
  186.5 202.7 %copy-start.3 = (bf16[128,129]{0,1:T(8,128)(2,1)S(1)}, bf16[128,129]{0,1:T(8,128)(2,1)}, u32[]{:S(2)}) copy-start(bf16[128,129]{0,1:T(8,128)(2,1)} %get-tuple-element.135) | copy-start | bytes 99076
  186.5 204.8 %copy-start.1 = (bf16[256,1024]{1,0:T(8,128)(2,1)S(1)}, bf16[256,1024]{1,0:T(8,128)(2,1)}, u32[]{:S(2)}) copy-start(bf16[256,1024]{1,0:T(8,128)(2,1)} %multiply_convert_fusion) | copy-start | bytes 1572868
  186.5 204.8 %copy-start.4 = (f32[1024]{0:T(1024)S(1)}, f32[1024]{0:T(1024)}, u32[]{:S(2)}) copy-start(f32[1024]{0:T(1024)} %param.26) | copy-start | bytes 12292
Sparse Core Ops, SparseCore 0:
  76.5 86.9 all-gather.1
  399.8 27.5 reduce-scatter.1
